TPU v7x, 512 devices: a whole 4x8x8 slice. The times are simulated.
512 devices in a mesh: row: 16 (over y, x_hi), col: 32 (over z, x_lo, core).
Axes of the slice: x: 4 (x_hi: 2, x_lo: 2; x = x_hi * 2 + x_lo), y: 8, z: 8, core: 2. Of those that a mesh axis runs over, the one named last changes fastest.
Arguments:
- features: bfloat16 [32, 2048, 128], P('col'), may hold values from -6 to 6
- dst_features: bfloat16 [65536, 128], P(('row', 'col')), may hold values from -6 to 6
- w_self: bfloat16 [128, 256], replicated, may hold values from -0.5 to 0.5
- w_neigh: bfloat16 [128, 256], replicated, may hold values from -0.5 to 0.5
- cotangent: bfloat16 [65536, 256], P(('row', 'col')), may hold values from -6 to 6
- block_values: bfloat16 [16, 32, 32, 128, 128], P('row', 'col'), may hold values from -0.15625 to 0.15625
- block_rows: int32 [16, 32, 32], P('row', 'col'), may hold values from 0 to 31, as said below
- block_cols: int32 [16, 32, 32], P('row', 'col'), may hold values from 0 to 15
- block_counts: int32 [16, 32], P('row', 'col'), may hold values from 4 to 32, as said below
Outputs:
- output: bfloat16 [65536, 256], P(('row', 'col'))
- grad_w_self: float32 [128, 256], replicated
- grad_w_neigh: float32 [128, 256], replicated
- grad_features: float32 [32, 2048, 128], P('col', 'row')
Inputs may be any that keep to these rules, and one draw needn't show every extreme that they name: On one device the slots name distinct pairs of block_rows and block_cols, also in unused slots. `block_counts`: some device uses all 32 slots in every draw.
All inputs are finite; a program needn't handle non-finite values.
Results may differ from a plain program's by a relative error of at most 0.0052.
Values may be sent and summed in bfloat16 or wider, within the bound.
A program may use at most 64 MiB of HBM per device.

v0:
```python
import math
import jax
import jax.numpy as jnp
from jax import lax
from jax.sharding import PartitionSpec as P


def slot_products(block_vals, source_table, slot_index, einsum_form):
    return jnp.einsum(
        einsum_form, block_vals, source_table[slot_index], preferred_element_type=jnp.float32
    )


def per_device(
    features,
    dst_features,
    w_self,
    w_neigh,
    cotangent,
    block_values,
    block_rows,
    block_cols,
    block_counts,
):
    block_size = block_values.shape[-1]
    feat_width = features.shape[-1]
    local_rows = dst_features.shape[0]
    col_total = lax.axis_size("col")
    slab_blocks = local_rows * col_total // block_size
    source_table = features.reshape(-1, block_size, feat_width)
    source_count = source_table.shape[0]
    block_vals = block_values[0, 0]
    row_ids = block_rows[0, 0]
    col_ids = block_cols[0, 0]
    live_count = block_counts[0, 0]
    slot_total = row_ids.shape[0]
    live_mask = jnp.arange(slot_total, dtype=jnp.int32) < live_count
    row_hits = (
        (row_ids[None, :] == jnp.arange(slab_blocks, dtype=jnp.int32)[:, None]) & live_mask[None, :]
    ).astype(jnp.float32)
    forward_terms = slot_products(block_vals, source_table, col_ids, "sij,sjf->sif")
    summed = jnp.einsum("rs,sif->rif", row_hits, forward_terms, precision=lax.Precision.HIGHEST)
    agg_sum = lax.psum_scatter(
        summed.reshape(local_rows * lax.axis_size("col"), feat_width),
        "col",
        scatter_dimension=0,
        tiled=True,
    )
    aggregate = agg_sum.astype(jnp.bfloat16)
    pre_act = jnp.dot(dst_features, w_self, preferred_element_type=jnp.float32) + jnp.dot(
        aggregate, w_neigh, preferred_element_type=jnp.float32
    )
    sigmoid_pre = jax.nn.sigmoid(pre_act)
    output = (pre_act * sigmoid_pre).astype(jnp.bfloat16)
    grad_pre = (
        cotangent.astype(jnp.float32) * sigmoid_pre * (1.0 + pre_act * (1.0 - sigmoid_pre))
    ).astype(jnp.bfloat16)
    node_total = local_rows * lax.axis_size("row") * col_total
    scale_factor = 1.0 / math.sqrt(node_total)
    self_grad = jnp.einsum("nf,nh->fh", dst_features, grad_pre, preferred_element_type=jnp.float32)
    neigh_grad = jnp.einsum("nf,nh->fh", aggregate, grad_pre, preferred_element_type=jnp.float32)
    self_sum, neigh_sum = lax.psum((self_grad, neigh_grad), ("row", "col"))
    local_grad = jnp.einsum(
        "nh,fh->nf", grad_pre, w_neigh, preferred_element_type=jnp.float32
    ).astype(jnp.bfloat16)
    slab_grad = lax.all_gather(local_grad, "col", axis=0, tiled=True)
    grad_table = slab_grad.reshape(slab_blocks, block_size, feat_width)
    backward_terms = slot_products(block_vals, grad_table, row_ids, "sij,sif->sjf")
    col_hits = (
        (col_ids[None, :] == jnp.arange(source_count, dtype=jnp.int32)[:, None])
        & live_mask[None, :]
    ).astype(jnp.float32)
    source_terms = jnp.einsum(
        "cs,sjf->cjf", col_hits, backward_terms, precision=lax.Precision.HIGHEST
    ).reshape(-1, feat_width)
    source_part = lax.psum_scatter(source_terms, "row", scatter_dimension=0, tiled=True)
    return (
        output,
        self_sum * scale_factor,
        neigh_sum * scale_factor,
        source_part.reshape(1, -1, feat_width),
    )


def solution(mesh):
    placed = (
        P("col", None, None),
        P(("row", "col"), None),
        P(),
        P(),
        P(("row", "col"), None),
        P("row", "col", None, None, None),
        P("row", "col", None),
        P("row", "col", None),
        P("row", "col"),
    )
    return jax.shard_map(
        per_device,
        mesh=mesh,
        in_specs=placed,
        out_specs=(P(("row", "col"), None), P(), P(), P("col", "row", None)),
        check_vma=False,
    )
```

profile of v0, /device:TPU:16, one launch (start us, length us, event | category | flops | bytes accessed | tf_op | source)
XLA Modules:
  0.0 701.7 jit_solution(4395809418823105912)
XLA Ops:
  7.2 0.0 copy-start
  7.2 0.0 reduce-scatter.3.cloned.1.call-start
  8.0 0.7 fusion.21
  8.6 1.8 gather_fusion
  10.4 0.0 copy-done
  10.4 2.2 fusion.6
  12.7 0.0 copy-start.4
  12.7 2.4 copy.21
  15.1 0.0 copy-done.4
  15.1 1.1 fusion.2
  16.2 2.6 copy.16
  18.8 0.0 copy-start.1
  18.8 0.0 copy-start.2
  18.8 0.0 copy-start.3
  18.8 0.0 copy-start.6
  18.8 0.0 reduce-scatter.3.cloned.1.call-update
  18.8 0.0 all-gather.2.cloned.1.call-start
  18.8 0.7 copy-done.1
  19.5 0.1 copy-done.2
  19.6 0.1 fusion.23
  19.8 125.8 %reduce-scatter.3.cloned.1.call-done = f32[128,128]{1,0:T(8,128)} async-done(((f32[4096,128]{1,0:T(8,128)}), f32[128,128]{1,0:T(8,128)}) %reduce-scatter.3.cloned.1.call-update) | async-done | bytes 65552 | tf_op jit(solution)/shard_map/reduce_scatter | solution.py:43
  145.6 0.0 copy-done.3
  145.6 0.0 copy-done.6
  145.6 1.7 multiply_convert_fusion
  147.2 0.8 convolution_convert_fusion
  148.0 0.0 all-gather.2.cloned.1.call-update
  148.0 0.0 all-reduce.3.cloned.1.call-start
  148.1 0.8 convolution_bitcast_fusion
  149.0 1.7 fusion.8
  150.7 0.0 all-reduce.3.cloned.1.call-update
  150.7 0.0 reduce-scatter.5.cloned.1.call-start
  150.8 61.6 %all-gather.2.cloned.1.call-done = bf16[4096,128]{1,0:T(8,128)(2,1)} async-done(((bf16[128,128]{1,0:T(8,128)(2,1)}), bf16[4096,128]{1,0:T(8,128)(2,1)}) %all-gather.2.cloned.1.call-update) | async-done | bytes 1048592 | tf_op jit(solution)/shard_map/all_gather | solution.py:66
  212.3 2.0 gather_fusion.1
  214.3 1.9 fusion.4
  216.2 0.0 copy-start.5
  216.2 2.4 copy.23
  218.6 0.0 copy-done.5
  218.6 0.8 fusion
  219.4 1.3 copy.18
  220.7 0.0 reduce-scatter.5.cloned.1.call-update
  220.8 265.3 %all-reduce.3.cloned.1.call-done = (f32[128,256]{0,1:T(8,128)}, f32[128,256]{0,1:T(8,128)}) async-done(((f32[128,256]{0,1:T(8,128)}, f32[128,256]{0,1:T(8,128)}), (f32[128,256]{0,1:T(8,128)}, f32[128,256]{0,1:T(8,128)})) %all-reduce.3.cloned.1.call-update) | async-done | bytes 262160 | tf_op jit(solution)/shard_map/psum | solution.py:62
  486.1 1.0 broadcast_multiply_fusion
  487.1 0.8 copy.20
  487.8 0.8 copy.19
  488.6 206.6 %reduce-scatter.5.cloned.1.call-done = f32[128,128]{1,0:T(8,128)} async-done(((f32[2048,128]{1,0:T(8,128)}), f32[128,128]{1,0:T(8,128)}) %reduce-scatter.5.cloned.1.call-update) | async-done | bytes 65552 | tf_op jit(solution)/shard_map/reduce_scatter | solution.py:76
  (4 shorter events, 0.0 us)
Async XLA Ops:
  7.2 3.3 copy-start
  7.2 138.4 %reduce-scatter.3.cloned.1.call-start = ((), (), s32[]{:S(2)}) async-start(), calls=%async_computation.2 | async-start | bytes 2162688 | tf_op jit(solution)/shard_map/reduce_scatter | solution.py:43
  12.7 2.4 copy-start.4
  18.8 0.8 copy-start.1
  18.8 0.9 copy-start.2
  18.8 126.8 %copy-start.3 = (bf16[128,256]{1,0:T(8,128)(2,1)S(1)}, bf16[128,256]{1,0:T(8,128)(2,1)}, u32[]{:S(2)}) copy-start(bf16[128,256]{1,0:T(8,128)(2,1)} %param.12) | copy-start | bytes 196612
  18.8 126.8 %copy-start.6 = (bf16[128,256]{1,0:T(8,128)(2,1)S(1)}, bf16[128,256]{1,0:T(8,128)(2,1)}, u32[]{:S(2)}) copy-start(bf16[128,256]{1,0:T(8,128)(2,1)} %param.13) | copy-start | bytes 196612
  18.8 193.5 %all-gather.2.cloned.1.call-start = ((), (), s32[]{:S(2)}) async-start(), calls=%async_computation.3 | async-start | bytes 1081344 | tf_op jit(solution)/shard_map/all_gather | solution.py:66
  148.0 338.1 %all-reduce.3.cloned.1.call-start = ((), (), s32[]{:S(2)}) async-start(), calls=%async_computation.5 | async-start | bytes 524288 | tf_op jit(solution)/shard_map/psum | solution.py:62
  150.7 544.5 %reduce-scatter.5.cloned.1.call-start = ((), (), s32[]{:S(2)}) async-start(), calls=%async_computation.4 | async-start | bytes 1114112 | tf_op jit(solution)/shard_map/reduce_scatter | solution.py:76
  216.2 2.4 copy-start.5
Sparse Core Ops, SparseCore 0:
  18.9 126.5 reduce-scatter.2
  148.5 63.7 all-gather.1
  218.9 267.1 all-reduce.2
  490.9 204.2 reduce-scatter.4
where the time goes:
time: 702 us
  waiting for transfers between devices  659 us (94%)
  local copies, waits for them, and re-layouts  14.7 us (2%)
  between operations  14.6 us (2%)
  matrix products  11.2 us (2%)
    psum x1, waiting for transfers between devices, per_device(): self_sum, neigh_sum = lax.psum((self_grad, neigh_grad), ('row', 'col'))  265 us
    reduce_scatter x1, waiting for transfers between devices, per_device(): lax.psum_scatter(source_terms, 'row', scatter_dimension=0, tiled=True)  207 us
    reduce_scatter x1, waiting for transfers between devices, per_device(): lax.psum_scatter(summed.reshape(local_rows * lax.axis_size('col'), feat_w...  126 us
    all_gather x1, waiting for transfers between devices, per_device(): slab_grad = lax.all_gather(local_grad, 'col', axis=0, tiled=True)  61.6 us
  transfers between devices with their start and end apart: 4, of which 4 were waited for; matrix products, arithmetic and copies ran while one was open for 2% of the time, Pallas kernels for 0%

commit v1 on v0

--- a/solution.py
+++ b/solution.py
@@ -59,7 +59,7 @@
     scale_factor = 1.0 / math.sqrt(node_total)
     self_grad = jnp.einsum("nf,nh->fh", dst_features, grad_pre, preferred_element_type=jnp.float32)
     neigh_grad = jnp.einsum("nf,nh->fh", aggregate, grad_pre, preferred_element_type=jnp.float32)
-    self_sum, neigh_sum = lax.psum((self_grad, neigh_grad), ("row", "col"))
+    self_sum, neigh_sum = lax.psum(lax.psum((self_grad, neigh_grad), "col"), "row")
     local_grad = jnp.einsum(
         "nh,fh->nf", grad_pre, w_neigh, preferred_element_type=jnp.float32
     ).astype(jnp.bfloat16)

time: 702 us -> 829 us (1.18)
  waiting for transfers between devices: 659 us -> 786 us
    psum x1 -> x2, waiting for transfers between devices: 265 us -> 380 us  [the longest x1 225 us: per_device(): lax.psum((self_grad, neigh_grad), 'col')]
  transfers between devices with their start and end apart: 4 -> 5, of which waited for: 4 -> 5; matrix products, arithmetic and copies ran while one was open for 2% -> 1% of each run, Pallas kernels for 0% -> 0%
where the time goes in v1:
time: 829 us
  waiting for transfers between devices  786 us (95%)
  local copies, waits for them, and re-layouts  14.7 us (2%)
  between operations  14.6 us (2%)
  matrix products  11.2 us (1%)
    psum x1, waiting for transfers between devices, per_device(): lax.psum((self_grad, neigh_grad), 'col')  225 us
    reduce_scatter x1, waiting for transfers between devices, per_device(): lax.psum_scatter(source_terms, 'row', scatter_dimension=0, tiled=True)  211 us
    psum x1, waiting for transfers between devices, per_device(): lax.psum(lax.psum((self_grad, neigh_grad), 'col'), 'row')  155 us
    reduce_scatter x1, waiting for transfers between devices, per_device(): lax.psum_scatter(summed.reshape(local_rows * lax.axis_size('col'), feat_w...  126 us
    all_gather x1, waiting for transfers between devices, per_device(): slab_grad = lax.all_gather(local_grad, 'col', axis=0, tiled=True)  69.5 us
  transfers between devices with their start and end apart: 5, of which 5 were waited for; matrix products, arithmetic and copies ran while one was open for 1% of the time, Pallas kernels for 0%

profile of v1, /device:TPU:16, one launch (start us, length us, event | category | flops | bytes accessed | tf_op | source)
XLA Modules:
  0.0 828.7 jit_solution(3565755258656175561)
XLA Ops:
  7.2 0.0 copy-start
  7.2 0.0 reduce-scatter.3.cloned.1.call-start
  8.0 0.7 fusion.21
  8.6 1.8 gather_fusion
  10.4 0.0 copy-done
  10.4 2.2 fusion.6
  12.7 0.0 copy-start.4
  12.7 2.4 copy.21
  15.0 0.0 copy-done.4
  15.1 1.1 fusion.2
  16.2 2.5 copy.16
  18.7 0.0 copy-start.1
  18.7 0.0 copy-start.2
  18.7 0.0 copy-start.3
  18.8 0.0 copy-start.6
  18.8 0.0 reduce-scatter.3.cloned.1.call-update
  18.8 0.0 all-reduce.5.cloned.1.call-start
  18.8 0.7 copy-done.1
  19.5 0.1 copy-done.2
  19.6 0.1 fusion.23
  19.7 125.8 %reduce-scatter.3.cloned.1.call-done = f32[128,128]{1,0:T(8,128)} async-done(((f32[4096,128]{1,0:T(8,128)}), f32[128,128]{1,0:T(8,128)}) %reduce-scatter.3.cloned.1.call-update) | async-done | bytes 65552 | tf_op jit(solution)/shard_map/reduce_scatter | solution.py:43
  145.5 0.0 copy-done.3
  145.5 0.0 copy-done.6
  145.5 1.7 multiply_convert_fusion
  147.2 0.8 convolution_bitcast_fusion
  148.1 1.7 fusion.8
  149.8 0.0 all-reduce.5.cloned.1.call-update
  149.8 0.0 all-gather.2.cloned.1.call-start
  149.9 0.8 convolution_convert_fusion
  150.6 0.0 all-gather.2.cloned.1.call-update
  150.7 0.0 all-reduce.7.cloned.1.call-start
  150.7 225.0 %all-reduce.5.cloned.1.call-done = (f32[128,256]{0,1:T(8,128)}, f32[128,256]{0,1:T(8,128)}) async-done(((f32[128,256]{0,1:T(8,128)}, f32[128,256]{0,1:T(8,128)}), (f32[128,256]{0,1:T(8,128)}, f32[128,256]{0,1:T(8,128)})) %all-reduce.5.cloned.1.call-update) | async-done | bytes 262160 | tf_op jit(solution)/shard_map/psum | solution.py:62
  375.7 0.0 all-reduce.7.cloned.1.call-update
  375.7 0.0 reduce-scatter.5.cloned.1.call-start
  375.8 69.5 %all-gather.2.cloned.1.call-done = bf16[4096,128]{1,0:T(8,128)(2,1)} async-done(((bf16[128,128]{1,0:T(8,128)(2,1)}), bf16[4096,128]{1,0:T(8,128)(2,1)}) %all-gather.2.cloned.1.call-update) | async-done | bytes 1048592 | tf_op jit(solution)/shard_map/all_gather | solution.py:66
  445.3 2.0 gather_fusion.1
  447.3 1.9 fusion.4
  449.1 0.0 copy-start.5
  449.1 2.4 copy.23
  451.5 0.0 copy-done.5
  451.5 0.8 fusion
  452.4 1.3 copy.18
  453.7 0.0 reduce-scatter.5.cloned.1.call-update
  453.7 155.3 %all-reduce.7.cloned.1.call-done = (f32[128,256]{0,1:T(8,128)}, f32[128,256]{0,1:T(8,128)}) async-done(((f32[128,256]{0,1:T(8,128)}, f32[128,256]{0,1:T(8,128)}), (f32[128,256]{0,1:T(8,128)}, f32[128,256]{0,1:T(8,128)})) %all-reduce.7.cloned.1.call-update) | async-done | bytes 262160 | tf_op jit(solution)/shard_map/psum | solution.py:62
  609.0 1.0 broadcast_multiply_fusion
  609.9 0.8 copy.20
  610.7 0.8 copy.19
  611.5 210.7 %reduce-scatter.5.cloned.1.call-done = f32[128,128]{1,0:T(8,128)} async-done(((f32[2048,128]{1,0:T(8,128)}), f32[128,128]{1,0:T(8,128)}) %reduce-scatter.5.cloned.1.call-update) | async-done | bytes 65552 | tf_op jit(solution)/shard_map/reduce_scatter | solution.py:76
  (4 shorter events, 0.0 us)
Async XLA Ops:
  7.2 3.3 copy-start
  7.2 138.4 %reduce-scatter.3.cloned.1.call-start = ((), (), s32[]{:S(2)}) async-start(), calls=%async_computation.2 | async-start | bytes 2162688 | tf_op jit(solution)/shard_map/reduce_scatter | solution.py:43
  12.7 2.4 copy-start.4
  18.7 0.8 copy-start.1
  18.7 0.9 copy-start.2
  18.7 126.8 %copy-start.3 = (bf16[128,256]{1,0:T(8,128)(2,1)S(1)}, bf16[128,256]{1,0:T(8,128)(2,1)}, u32[]{:S(2)}) copy-start(bf16[128,256]{1,0:T(8,128)(2,1)} %param.12) | copy-start | bytes 196612
  18.8 126.8 %copy-start.6 = (bf16[128,256]{1,0:T(8,128)(2,1)S(1)}, bf16[128,256]{1,0:T(8,128)(2,1)}, u32[]{:S(2)}) copy-start(bf16[128,256]{1,0:T(8,128)(2,1)} %param.13) | copy-start | bytes 196612
  18.8 356.9 %all-reduce.5.cloned.1.call-start = ((), (), s32[]{:S(2)}) async-start(), calls=%async_computation.5 | async-start | bytes 524288 | tf_op jit(solution)/shard_map/psum | solution.py:62
  149.8 295.5 %all-gather.2.cloned.1.call-start = ((), (), s32[]{:S(2)}) async-start(), calls=%async_computation.3 | async-start | bytes 1081344 | tf_op jit(solution)/shard_map/all_gather | solution.py:66
  150.7 458.3 %all-reduce.7.cloned.1.call-start = ((), (), s32[]{:S(2)}) async-start(), calls=%async_computation.6 | async-start | bytes 524288 | tf_op jit(solution)/shard_map/psum | solution.py:62
  375.7 446.4 %reduce-scatter.5.cloned.1.call-start = ((), (), s32[]{:S(2)}) async-start(), calls=%async_computation.4 | async-start | bytes 1114112 | tf_op jit(solution)/shard_map/reduce_scatter | solution.py:76
  449.1 2.4 copy-start.5
Sparse Core Ops, SparseCore 0:
  18.9 126.5 reduce-scatter.2
  149.9 225.7 all-reduce.4
  378.4 66.7 all-gather.1
  448.1 160.8 all-reduce.6
  614.4 207.6 reduce-scatter.4

commit v2 on v0

--- a/solution.py
+++ b/solution.py
@@ -63,7 +63,9 @@
     local_grad = jnp.einsum(
         "nh,fh->nf", grad_pre, w_neigh, preferred_element_type=jnp.float32
     ).astype(jnp.bfloat16)
-    slab_grad = lax.all_gather(local_grad, "col", axis=0, tiled=True)
+    slab_grad = jnp.concatenate(
+        lax.all_to_all(jnp.stack([local_grad] * lax.axis_size("col")), "col", 0, 0), axis=0
+    )
     grad_table = slab_grad.reshape(slab_blocks, block_size, feat_width)
     backward_terms = slot_products(block_vals, grad_table, row_ids, "sij,sif->sjf")
     col_hits = (

time: 702 us -> 645 us (0.919)
  waiting for transfers between devices: 659 us -> 600 us
    all_gather x1 -> x0, waiting for transfers between devices: 61.6 us -> none  [per_device(): slab_grad = lax.all_gather(local_grad, 'col', axis=0, tiled=True)]
    all_to_all x0 -> x1, waiting for transfers between devices: none -> 27.3 us  [per_device(): lax.all_to_all(jnp.stack([local_grad] * lax.axis_size('col')), 'col', 0, 0)]
    psum x1, waiting for transfers between devices: 265 us -> 240 us  [per_device(): self_sum, neigh_sum = lax.psum((self_grad, neigh_grad), ('row', 'col'))]
where the time goes in v2:
time: 645 us
  waiting for transfers between devices  600 us (93%)
  local copies, waits for them, and re-layouts  14.8 us (2%)
  between operations  14.6 us (2%)
  matrix products  9.82 us (2%)
    psum x1, waiting for transfers between devices, per_device(): self_sum, neigh_sum = lax.psum((self_grad, neigh_grad), ('row', 'col'))  240 us
    reduce_scatter x1, waiting for transfers between devices, per_device(): lax.psum_scatter(source_terms, 'row', scatter_dimension=0, tiled=True)  207 us
    reduce_scatter x1, waiting for transfers between devices, per_device(): lax.psum_scatter(summed.reshape(local_rows * lax.axis_size('col'), feat_w...  126 us
    all_to_all x1, waiting for transfers between devices, per_device(): lax.all_to_all(jnp.stack([local_grad] * lax.axis_size('col')), 'col', 0, 0)  27.3 us
  transfers between devices with their start and end apart: 4, of which 4 were waited for; matrix products, arithmetic and copies ran while one was open for 2% of the time, Pallas kernels for 0%

profile of v2, /device:TPU:16, one launch (start us, length us, event | category | flops | bytes accessed | tf_op | source)
XLA Modules:
  0.0 644.7 jit_solution(5515891633217700515)
XLA Ops:
  7.2 0.0 copy-start
  7.2 0.0 reduce-scatter.3.cloned.1.call-start
  8.0 0.7 fusion.21
  8.6 1.8 gather_fusion
  10.4 0.0 copy-done
  10.4 2.2 fusion.6
  12.7 0.0 copy-start.5
  12.7 2.4 copy.21
  15.1 0.0 copy-done.5
  15.1 1.1 fusion.2
  16.2 2.6 copy.16
  18.8 0.0 copy-start.1
  18.8 0.0 copy-start.2
  18.8 0.0 copy-start.3
  18.8 0.0 copy-start.7
  18.8 0.0 reduce-scatter.3.cloned.1.call-update
  18.8 0.7 copy-done.1
  19.5 0.1 copy-done.2
  19.6 0.1 fusion.23
  19.8 125.8 %reduce-scatter.3.cloned.1.call-done = f32[128,128]{1,0:T(8,128)} async-done(((f32[4096,128]{1,0:T(8,128)}), f32[128,128]{1,0:T(8,128)}) %reduce-scatter.3.cloned.1.call-update) | async-done | bytes 65552 | tf_op jit(solution)/shard_map/reduce_scatter | solution.py:43
  145.6 0.0 copy-done.3
  145.6 0.0 copy-done.7
  145.6 0.0 copy-start.4
  145.6 1.7 multiply_convert_fusion
  147.3 0.2 convolution_convert_fusion
  147.5 1.2 stack.2
  148.7 4.1 all-to-all-start
  152.9 0.0 all-reduce.3.cloned.1.call-start
  152.9 0.9 convolution_bitcast_fusion
  153.8 0.0 copy-done.4
  153.8 0.9 fusion.8
  154.7 0.0 all-reduce.3.cloned.1.call-update
  154.7 0.0 reduce-scatter.5.cloned.1.call-start
  154.7 27.3 %all-to-all-done = bf16[32,128,128]{2,1,0:T(8,128)(2,1)S(1)} async-done(((bf16[32,128,128]{2,1,0:T(8,128)(2,1)}), bf16[32,128,128]{2,1,0:T(8,128)(2,1)S(1)}, u32[]{:S(2)}, u32[]{:S(2)}) %all-to-all-start) | async-done | bytes 1048608 | tf_op jit(solution)/shard_map/all_to_all | solution.py:67
  182.0 0.7 gather_fusion.1
  182.8 1.9 fusion.4
  184.7 0.0 copy-start.6
  184.7 2.4 copy.23
  187.0 0.0 copy-done.6
  187.1 0.8 fusion
  187.9 1.3 copy.18
  189.2 0.0 reduce-scatter.5.cloned.1.call-update
  189.2 239.7 %all-reduce.3.cloned.1.call-done = (f32[128,256]{0,1:T(8,128)}, f32[128,256]{0,1:T(8,128)}) async-done(((f32[128,256]{0,1:T(8,128)}, f32[128,256]{0,1:T(8,128)}), (f32[128,256]{0,1:T(8,128)}, f32[128,256]{0,1:T(8,128)})) %all-reduce.3.cloned.1.call-update) | async-done | bytes 262160 | tf_op jit(solution)/shard_map/psum | solution.py:62
  428.9 1.0 broadcast_multiply_fusion
  429.9 0.8 copy.20
  430.7 0.8 copy.19
  431.4 206.7 %reduce-scatter.5.cloned.1.call-done = f32[128,128]{1,0:T(8,128)} async-done(((f32[2048,128]{1,0:T(8,128)}), f32[128,128]{1,0:T(8,128)}) %reduce-scatter.5.cloned.1.call-update) | async-done | bytes 65552 | tf_op jit(solution)/shard_map/reduce_scatter | solution.py:78
  (4 shorter events, 0.0 us)
Async XLA Ops:
  7.2 3.3 copy-start
  7.2 138.4 %reduce-scatter.3.cloned.1.call-start = ((), (), s32[]{:S(2)}) async-start(), calls=%async_computation.3 | async-start | bytes 2162688 | tf_op jit(solution)/shard_map/reduce_scatter | solution.py:43
  12.7 2.4 copy-start.5
  18.8 0.8 copy-start.1
  18.8 0.9 copy-start.2
  18.8 126.8 %copy-start.3 = (bf16[128,256]{1,0:T(8,128)(2,1)S(1)}, bf16[128,256]{1,0:T(8,128)(2,1)}, u32[]{:S(2)}) copy-start(bf16[128,256]{1,0:T(8,128)(2,1)} %param.12) | copy-start | bytes 196612
  18.8 126.8 %copy-start.7 = (bf16[128,256]{1,0:T(8,128)(2,1)S(1)}, bf16[128,256]{1,0:T(8,128)(2,1)}, u32[]{:S(2)}) copy-start(bf16[128,256]{1,0:T(8,128)(2,1)} %param.13) | copy-start | bytes 196612
  145.6 8.2 %copy-start.4 = (f32[128,128]{1,0:T(8,128)S(1)}, f32[128,128]{1,0:T(8,128)}, u32[]{:S(2)}) copy-start(f32[128,128]{1,0:T(8,128)} %reduce-scatter.3.cloned.1.call-done) | copy-start | bytes 196612
  148.7 33.3 %all-to-all-start = ((bf16[32,128,128]{2,1,0:T(8,128)(2,1)}), bf16[32,128,128]{2,1,0:T(8,128)(2,1)S(1)}, u32[]{:S(2)}, u32[]{:S(2)}) async-start(bf16[32,128,128]{2,1,0:T(8,128)(2,1)} %stack.2), calls=%async_computation.1 | async-start | bytes 2097152 | tf_op jit(solution)/shard_map/all_to_all | solution.py:67
  152.9 276.1 %all-reduce.3.cloned.1.call-start = ((), (), s32[]{:S(2)}) async-start(), calls=%async_computation.5 | async-start | bytes 524288 | tf_op jit(solution)/shard_map/psum | solution.py:62
  154.7 483.5 %reduce-scatter.5.cloned.1.call-start = ((), (), s32[]{:S(2)}) async-start(), calls=%async_computation.4 | async-start | bytes 1114112 | tf_op jit(solution)/shard_map/reduce_scatter | solution.py:78
  184.7 2.4 copy-start.6
Sparse Core Ops, SparseCore 0:
  18.9 126.6 reduce-scatter.2
  160.3 268.6 all-reduce.2
  433.9 204.1 reduce-scatter.4
